TPU v7x, 128 devices: a whole 4x4x4 slice. The times are simulated.
128 devices in a mesh: row: 16 (over x, z), col: 8 (over y, core).
Axes of the slice: x: 4, y: 4, z: 4, core: 2. Of those that a mesh axis runs over, the one named last changes fastest.
Arguments:
- attn: bfloat16 [2048, 16384], P('col', 'row'), may hold values from -6 to 6
- grad_out: bfloat16 [2048, 16384], P('row', 'col'), may hold values from -0.119628906 to 0.119628906
- weight: bfloat16 [16384, 16384], P('row', 'col'), may hold values from -2.09375 to 2.09375
- momentum: bfloat16 [16384, 16384], P('row', 'col'), may hold values from -3 to 3
Outputs:
- grad_in: bfloat16 [2048, 16384], P('col', 'row')
- new_weight: bfloat16 [16384, 16384], P('row', 'col')
- new_momentum: bfloat16 [16384, 16384], P('row', 'col')
All inputs are finite; a program needn't handle non-finite values.
Results may differ from a plain program's by a relative error of at most 0.014.
Values may be sent and summed in bfloat16 or wider, within the bound.
A program may use at most 128 MiB of HBM per device.

v0:
```python
import jax
import jax.numpy as jnp
from jax import lax
from jax.sharding import PartitionSpec as P


def shards(attn, grad_out, weight, momentum):
    contract_rows = (((0,), (0,)), ((), ()))
    contract_cols = (((1,), (1,)), ((), ()))
    grads_all = lax.all_gather(grad_out, "row", axis=0, tiled=True)
    rows_here = grads_all
    grad_w = lax.dot_general(
        lax.all_gather(attn, "col", axis=0, tiled=True),
        rows_here,
        contract_rows,
        preferred_element_type=jnp.float32,
    )
    rows_here = grads_all
    grad_in = lax.psum_scatter(
        lax.dot_general(
            rows_here, weight, contract_cols, preferred_element_type=jnp.float32
        ).astype(jnp.bfloat16),
        "col",
        scatter_dimension=0,
        tiled=True,
    )
    mom = 0.9 * momentum.astype(jnp.float32) + grad_w
    new_weight = (weight.astype(jnp.float32) - 0.25 * mom).astype(jnp.bfloat16)
    return (grad_in, new_weight, mom.astype(jnp.bfloat16))


def solution(mesh):
    in_specs = (P("col", "row"), P("row", "col"), P("row", "col"), P("row", "col"))
    out_specs = (P("col", "row"), P("row", "col"), P("row", "col"))
    return jax.shard_map(shards, mesh=mesh, in_specs=in_specs, out_specs=out_specs, check_vma=False)
```

profile of v0, /device:TPU:1, one launch (start us, length us, event | category | flops | bytes accessed | tf_op | source)
XLA Modules:
  0.0 162.2 jit_solution(2336899763222875752)
XLA Ops:
  7.2 0.0 all-gather.3.cloned.1.call-start
  7.2 0.7 all-gather.3.cloned.1.call-update
  7.9 0.0 all-gather.5.cloned.1.call-start
  7.9 0.7 all-gather.5.cloned.1.call-update
  8.6 0.0 reduce-scatter.2.cloned.1.call-start
  8.7 75.4 %all-gather.3.cloned.1.call-done = bf16[2048,2048]{1,0:T(8,128)(2,1)} async-done(((bf16[128,2048]{1,0:T(8,128)(2,1)}), bf16[2048,2048]{1,0:T(8,128)(2,1)}) %all-gather.3.cloned.1.call-update) | async-done | bytes 8388624 | tf_op jit(solution)/shard_map/all_gather | solution.py:10
  84.1 13.8 %convolution_convert_fusion = bf16[2048,1024]{1,0:T(8,128)(2,1)} fusion(bf16[2048,2048]{1,0:T(8,128)(2,1)} %all-gather.3.cloned.1.call-done, bf16[1024,2048]{1,0:T(8,128)(2,1)} %param.6), kind=kOutput, calls=%fused_computation.3 | convolution fusion | flops 8592031744 | bytes 16777216 | tf_op jit(solution)/shard_map/dot_general | solution.py:20
  98.0 0.0 reduce-scatter.2.cloned.1.call-update
  98.0 20.1 %all-gather.5.cloned.1.call-done = bf16[2048,1024]{1,0:T(8,128)(2,1)} async-done(((bf16[256,1024]{1,0:T(8,128)(2,1)}), bf16[2048,1024]{1,0:T(8,128)(2,1)}) %all-gather.5.cloned.1.call-update) | async-done | bytes 4194320 | tf_op jit(solution)/shard_map/all_gather | solution.py:13
  118.1 17.7 %fusion = (bf16[1024,2048]{1,0:T(8,128)(2,1)}, bf16[1024,2048]{1,0:T(8,128)(2,1)}) fusion(bf16[1024,2048]{1,0:T(8,128)(2,1)} %param.7, bf16[1024,2048]{1,0:T(8,128)(2,1)} %param.6, bf16[2048,1024]{1,0:T(8,128)(2,1)} %all-gather.5.cloned.1.call-done, bf16[2048,2048]{1,0:T(8,128)(2,1)} %all-gather.3.cloned.1.call-done), kind=kOutput, calls=%fused_computation.2 | convolution fusion | flops 8606711808 | bytes 29360128 | tf_op jit(solution)/shard_map/dot_general | solution.py:12
  135.8 19.9 %reduce-scatter.2.cloned.1.call-done = bf16[256,1024]{1,0:T(8,128)(2,1)} async-done(((bf16[2048,1024]{1,0:T(8,128)(2,1)}), bf16[256,1024]{1,0:T(8,128)(2,1)}) %reduce-scatter.2.cloned.1.call-update) | async-done | bytes 524304 | tf_op jit(solution)/shard_map/reduce_scatter | solution.py:19
Async XLA Ops:
  7.2 77.0 %all-gather.3.cloned.1.call-start = ((), (), s32[]{:S(2)}) async-start(), calls=%async_computation.1 | async-start | bytes 8912896 | tf_op jit(solution)/shard_map/all_gather | solution.py:10
  7.9 110.2 %all-gather.5.cloned.1.call-start = ((), (), s32[]{:S(2)}) async-start(), calls=%async_computation.3 | async-start | bytes 4718592 | tf_op jit(solution)/shard_map/all_gather | solution.py:13
  8.6 147.0 %reduce-scatter.2.cloned.1.call-start = ((), (), s32[]{:S(2)}) async-start(), calls=%async_computation.2 | async-start | bytes 4718592 | tf_op jit(solution)/shard_map/reduce_scatter | solution.py:19
Sparse Core Ops, SparseCore 0:
  10.1 73.9 all-gather.2
  85.8 32.1 all-gather.4
  121.0 34.5 reduce-scatter.1
where the time goes:
time: 164 us; the launch traced here: 162 us
  waiting for transfers between devices  117 us (71%)
  matrix products  31.6 us (19%)
  between operations  13.7 us (8%)
    all_gather x1, waiting for transfers between devices, shards(): grads_all = lax.all_gather(grad_out, 'row', axis=0, tiled=True)  75.4 us
    all_gather x1, waiting for transfers between devices, shards(): lax.all_gather(attn, 'col', axis=0, tiled=True)  20.1 us
    reduce_scatter x1, waiting for transfers between devices, shards(): lax.psum_scatter(lax.dot_general(rows_here, weight, contract_cols, prefer...  19.9 us
    dot_general x1, matrix products, shards(): lax.dot_general(lax.all_gather(attn, 'col', axis=0, tiled=True), rows_her...  17.7 us
    dot_general x1, matrix products, shards(): lax.dot_general(rows_here, weight, contract_cols, preferred_element_type=...  13.8 us
  transfers between devices with their start and end apart: 3, of which 3 were waited for; matrix products, arithmetic and copies ran while one was open for 19% of the time, Pallas kernels for 0%

commit v1 on v0

v1 whole, which is shorter than its diff:
```python
import jax
import jax.numpy as jnp
from jax import lax
from jax.experimental import pallas as pl
from jax.experimental.pallas import tpu as pltpu
from jax.sharding import PartitionSpec as P

MESH = pl.DeviceIdType.MESH
BF = jnp.bfloat16
F32 = jnp.float32
NT = (((1,), (1,)), ((), ()))
TN = (((0,), (0,)), ((), ()))

GROUPS = [
    [(0, 0, 0), (0, 1, 0), (0, -1, 0), (0, 2, 0)],
    [(1, 0, 0), (1, 1, 0), (1, -1, 0), (1, 2, 0)],
    [(0, 0, 1), (0, 0, -1), (1, 0, 1), (1, 0, -1)],
    [(0, 1, 1), (0, 1, -1), (1, 1, 1), (1, 1, -1)],
    [(0, 2, 1), (0, 2, -1), (1, 2, 1), (1, 2, -1)],
    [(0, -1, 1), (0, -1, -1), (1, -1, 1), (1, -1, -1)],
    [(0, 0, 2), (0, 2, 2), (1, 0, 2), (1, 2, 2)],
    [(0, 1, 2), (0, -1, 2), (1, 1, 2), (1, -1, 2)],
]
SLOT = {piece: (g, j) for g, group in enumerate(GROUPS) for j, piece in enumerate(group)}
DU = (0, 1, 2, -1)


def kernel(attn, gout, w_in, m_in, gin_o, nw_o, nm_o,
           G, A, W, M, acc, AG, part, sib, mid, fin,
           ag_s, ag_r, at_s, at_r, x_s, x_r, y_s, mid_r, fin_r, loc):
    r = lax.axis_index("row")
    c = lax.axis_index("col")
    x, z, y, k = r // 4, r % 4, c // 2, c % 2

    def at(dx=0, dz=0, dy=0, dk=0):
        return {
            "row": ((x + dx + 4) % 4) * 4 + (z + dz + 4) % 4,
            "col": ((y + dy + 4) % 4) * 2 + (k + dk) % 2,
        }

    def along(half, first, s):
        return at(dx=s) if (half == 0) == first else at(dz=s)

    def slot(piece, lo=0, n=64):
        g, j = SLOT[piece]
        return G.at[g // 2, pl.ds((g % 2) * 256 + j * 64 + lo, n), :]

    def remote(src, dst, ss, rs, dev):
        return pltpu.make_async_remote_copy(
            src_ref=src, dst_ref=dst, send_sem=ss, recv_sem=rs,
            device_id=dev, device_id_type=MESH)

    locals_ = [
        pltpu.make_async_copy(gout.at[pl.ds(0, 64), :], slot((0, 0, 0)), loc.at[0]),
        pltpu.make_async_copy(gout.at[pl.ds(64, 64), :], slot((1, 0, 0)), loc.at[1]),
        pltpu.make_async_copy(attn, A.at[pl.ds(c * 256, 256), :], loc.at[2]),
        pltpu.make_async_copy(w_in, W, loc.at[3]),
        pltpu.make_async_copy(m_in, M, loc.at[4]),
    ]
    for copy in locals_:
        copy.start()

    ag = {}
    for h in (0, 1):
        own = gout.at[pl.ds(64 * h, 64), :]
        n = 20 * h
        for s in (1, -1):
            ag["P", h, s] = (own, slot((h, -s, 0)), along(h, True, s))
            q = 0 if s == 1 else 32
            ag["PF", h, s] = (slot((h, -s, 0), q, 32), slot((h, 2, 0), q, 32), along(h, True, s))
            for du in DU:
                src = own if du == 0 else slot((h, du, 0))
                ag["S", h, du, s] = (src, slot((h, du, -s)), along(h, False, s))
                ag["F", h, du, s] = (slot((h, du, -s), q, 32), slot((h, du, 2), q, 32), along(h, False, s))
    ag = {key: remote(src, dst, ag_s.at[i], ag_r.at[i], dev)
          for i, (key, (src, dst, dev)) in enumerate(ag.items())}

    def send(kind, *rest):
        for h in (0, 1):
            for s in (1, -1):
                ag[(kind, h, *rest, s)].start()

    def recv(kind, *rest):
        for h in (0, 1):
            for s in (1, -1):
                ag[(kind, h, *rest, s)].wait_recv()

    def block(dy, dk=0, lo=0, n=256):
        col = ((y + dy + 4) % 4) * 2 + (k + dk) % 2
        return A.at[pl.ds(pl.multiple_of(col * 256 + lo, 128), n), :]

    def attn_copy(i, src, dst, dev):
        return remote(src, dst, at_s.at[i], at_r.at[i], dev)

    up, down, other = at(dy=1), at(dy=-1), at(dk=1)
    a_own = {1: attn_copy(0, attn, block(0), up), -1: attn_copy(1, attn, block(0), down)}
    a_sib = attn_copy(2, attn, block(0), other)
    a_fwd = {1: attn_copy(3, block(-1, 0, 0, 128), block(-1, 0, 0, 128), up),
             -1: attn_copy(4, block(1, 0, 128, 128), block(1, 0, 128, 128), down)}
    a_pass = {1: attn_copy(5, block(-1), block(-1), other),
              -1: attn_copy(6, block(1), block(1), other)}
    a_last = {1: attn_copy(7, block(2, 0, 0, 128), block(2, 0, 0, 128), other),
              -1: attn_copy(8, block(2, 0, 128, 128), block(2, 0, 128, 128), other)}

    def place(g, j):
        h, du, dv = GROUPS[g][j]
        dx, dz = (du, dv) if h == 0 else (dv, du)
        xs, zs = (x + dx + 4) % 4, (z + dz + 4) % 4
        d = (xs - y + 4) % 4
        mine = zs // 2 == k
        o = (zs % 2) * 2 + h
        return 4 * g + j, xs * 512 + zs * 128 + 64 * h, d, mine, o

    def rows(g, j):
        return part.at[g, pl.ds(64 * j, 64), :]

    def to_sibling(g, j):
        p = 4 * g + j
        return remote(rows(g, j), sib.at[p], x_s.at[p], x_r.at[p], other)

    def to_mid(g, j, q):
        p = 4 * g + j
        return remote(part.at[g, pl.ds(64 * j, 64), pl.ds(512 * q, 512)], mid.at[p],
                      y_s.at[p, q], mid_r.at[p], up if q == 0 else down)

    def to_owner(g, j):
        p, _, d, _, o = place(g, j)
        q = (d == 3).astype(jnp.int32)
        dev = {"row": r, "col": ((y + 1 + 2 * q) % 4) * 2 + k}
        return remote(rows(g, j), fin.at[o, q], y_s.at[p, 0], fin_r.at[o, q], dev)

    def step1(g):
        for j in range(4):
            _, _, _, mine, _ = place(g, j)

            @pl.when(jnp.logical_not(mine))
            def _():
                to_sibling(g, j).start()

    def step2(g):
        for j in range(4):
            p, _, d, mine, _ = place(g, j)

            @pl.when(mine)
            def _():
                to_sibling(g, j).wait_recv()
                part[g, pl.ds(64 * j, 64), :] = (
                    part[g, pl.ds(64 * j, 64), :].astype(F32) + sib[p].astype(F32)).astype(BF)

                @pl.when(d == 2)
                def _():
                    to_mid(g, j, 0).start()
                    to_mid(g, j, 1).start()

    def step3(g):
        for j in range(4):
            p, _, d, mine, _ = place(g, j)

            @pl.when(jnp.logical_and(mine, d % 2 == 1))
            def _():
                q = (d == 3).astype(jnp.int32)
                to_mid(g, j, 0).wait_recv()
                f = pl.ds(pl.multiple_of(q * 512, 512), 512)
                part[g, pl.ds(64 * j, 64), f] = (
                    part[g, pl.ds(64 * j, 64), f].astype(F32) + mid[p].astype(F32)).astype(BF)
                to_owner(g, j).start()

    def step4(g):
        for j in range(4):
            _, _, d, mine, o = place(g, j)

            @pl.when(jnp.logical_and(mine, d == 0))
            def _():
                for q in (0, 1):
                    remote(rows(g, j), fin.at[o, q], y_s.at[4 * g + j, 0], fin_r.at[o, q], up).wait_recv()
                gin_o[pl.ds(pl.multiple_of(o * 64, 64), 64), :] = (
                    part[g, pl.ds(64 * j, 64), :].astype(F32)
                    + fin[o, 0].astype(F32) + fin[o, 1].astype(F32)).astype(BF)

    def drain(g):
        for j in range(4):
            _, _, d, mine, _ = place(g, j)

            @pl.when(jnp.logical_not(mine))
            def _():
                to_sibling(g, j).wait_send()

            @pl.when(jnp.logical_and(mine, d == 2))
            def _():
                to_mid(g, j, 0).wait_send()
                to_mid(g, j, 1).wait_send()

            @pl.when(jnp.logical_and(mine, d % 2 == 1))
            def _():
                to_owner(g, j).wait_send()

    def partial(g):
        def tile(n, _):
            n = pl.multiple_of(n * 512, 512)
            part[g, :, pl.ds(n, 512)] = lax.dot_general(
                G[g // 2, pl.ds((g % 2) * 256, 256), :], W[pl.ds(n, 512), :], NT,
                preferred_element_type=F32).astype(BF)
            return 0

        lax.fori_loop(0, 2, tile, 0)

    def collect(g):
        for j in range(4):
            _, token, _, _, _ = place(g, j)
            AG[pl.ds((g % 2) * 256 + 64 * j, 64), :] = A[pl.ds(pl.multiple_of(token, 64), 64), :]

    def grad_w(p, first, last):
        collect(2 * p)
        collect(2 * p + 1)

        def tile(i, _):
            f = pl.ds(pl.multiple_of(i * 256, 256), 256)
            t = lax.dot_general(AG[:, f], G[p], TN, preferred_element_type=F32)
            if not first:
                t = acc[f, :] + t
            if last:
                mom = 0.9 * M[f, :].astype(F32) + t
                nm_o[f, :] = mom.astype(BF)
                nw_o[f, :] = (W[f, :].astype(F32) - 0.25 * mom).astype(BF)
            else:
                acc[f, :] = t
            return 0

        lax.fori_loop(0, 4, tile, 0)

    barrier = pltpu.get_barrier_semaphore()
    neighbours = [at(dx=1), at(dx=-1), at(dz=1), at(dz=-1), up, down, other]
    for dev in neighbours:
        pl.semaphore_signal(barrier, inc=1, device_id=dev, device_id_type=MESH)
    pl.semaphore_wait(barrier, len(neighbours))

    send("P")
    for s in (1, -1):
        a_own[s].start()
    a_sib.start()
    send("S", 0)

    recv("P")
    send("PF")
    send("S", 1)
    for copy in locals_[:4]:
        copy.wait()

    recv("S", 0)
    for s in (1, -1):
        a_own[s].wait_recv()
        a_fwd[s].start()
    for s in (1, -1):
        a_pass[s].start()
    partial(2)
    recv("PF")
    send("S", 2)
    send("S", -1)
    send("F", 0)
    step1(2)
    partial(0)
    step1(0)
    step2(2)
    partial(1)
    step1(1)
    step2(0)
    step3(2)
    a_sib.wait_recv()
    for s in (1, -1):
        a_fwd[s].wait_recv()
        a_last[s].start()
    for s in (1, -1):
        a_pass[s].wait_recv()
    step2(1)
    for s in (1, -1):
        a_last[s].wait_recv()
    grad_w(0, True, False)
    step3(0)
    step3(1)
    recv("S", 1)
    partial(3)
    step1(3)
    step4(2)
    grad_w(1, False, False)
    step2(3)
    step4(0)
    step4(1)
    recv("S", 2)
    send("F", 2)
    send("F", 1)
    partial(4)
    step1(4)
    step3(3)
    recv("S", -1)
    send("F", -1)
    step2(4)
    partial(5)
    step1(5)
    step3(4)
    step4(3)
    grad_w(2, False, False)
    step2(5)
    step4(4)
    recv("F", 0)
    recv("F", 2)
    partial(6)
    step1(6)
    step3(5)
    step4(5)
    step2(6)
    recv("F", 1)
    recv("F", -1)
    partial(7)
    step1(7)
    step3(6)
    step2(7)
    step4(6)
    locals_[4].wait()
    step3(7)
    grad_w(3, False, True)
    step4(7)

    for copy in ag.values():
        copy.wait_send()
    for copies in (a_own, a_fwd, a_pass, a_last):
        for s in (1, -1):
            copies[s].wait_send()
    a_sib.wait_send()
    for g in range(8):
        drain(g)


def shards(attn, grad_out, weight, momentum):
    hbm = pl.BlockSpec(memory_space=pl.ANY)
    vmem = pl.BlockSpec(memory_space=pltpu.VMEM)
    dma = pltpu.SemaphoreType.DMA
    return pl.pallas_call(
        kernel,
        out_shape=(
            jax.ShapeDtypeStruct((256, 1024), BF),
            jax.ShapeDtypeStruct((1024, 2048), BF),
            jax.ShapeDtypeStruct((1024, 2048), BF),
        ),
        in_specs=[hbm] * 4,
        out_specs=(vmem,) * 3,
        scratch_shapes=[
            pltpu.VMEM((4, 512, 2048), BF),
            pltpu.VMEM((2048, 1024), BF),
            pltpu.VMEM((1024, 2048), BF),
            pltpu.VMEM((1024, 2048), BF),
            pltpu.VMEM((1024, 2048), F32),
            pltpu.VMEM((512, 1024), BF),
            pltpu.VMEM((8, 256, 1024), BF),
            pltpu.VMEM((32, 64, 1024), BF),
            pltpu.VMEM((32, 64, 512), BF),
            pltpu.VMEM((4, 2, 64, 1024), BF),
            dma((40,)), dma((40,)), dma((9,)), dma((9,)),
            dma((32,)), dma((32,)), dma((32, 2)), dma((32,)), dma((4, 2)), dma((5,)),
        ],
        compiler_params=pltpu.CompilerParams(
            collective_id=0, has_side_effects=True, vmem_limit_bytes=67043328),
        cost_estimate=pl.CostEstimate(flops=4 * 2048 * 1024 * 2048, bytes_accessed=17 << 20, transcendentals=0),
    )(attn, grad_out, weight, momentum)


def solution(mesh):
    in_specs = (P("col", "row"), P("row", "col"), P("row", "col"), P("row", "col"))
    out_specs = (P("col", "row"), P("row", "col"), P("row", "col"))
    return jax.shard_map(shards, mesh=mesh, in_specs=in_specs, out_specs=out_specs, check_vma=False)
```

time: 164 us -> 91.1 us (0.56)
  waiting for transfers between devices: 117 us -> 0 us
  Pallas kernels: 0 us -> 81.3 us
  matrix products: 31.6 us -> 0 us
  between operations: 13.7 us -> 0.64 us
  local copies, waits for them, and re-layouts: 0 us -> 8.82 us
    all_gather x2 -> x0, waiting for transfers between devices: 95.5 us -> none  [the longest x1 75.4 us: shards(): grads_all = lax.all_gather(grad_out, 'row', axis=0, tiled=True)]
    pallas_call x0 -> x1, Pallas kernels: none -> 81.3 us  [shards(): pl.pallas_call(kernel, out_shape=(jax.ShapeDtypeStruct((256, 1024), BF),...]
    dot_general x2 -> x0, matrix products: 31.6 us -> none  [the longest x1 17.7 us: shards(): lax.dot_general(lax.all_gather(attn, 'col', axis=0, tiled=True), rows_her...]
    reduce_scatter x1 -> x0, waiting for transfers between devices: 19.9 us -> none  [shards(): lax.psum_scatter(lax.dot_general(rows_here, weight, contract_cols, prefer...]
    unnamed x0 -> x5, local copies, waits for them, and re-layouts: none -> 8.82 us
  transfers between devices with their start and end apart: 3 -> 0, of which waited for: 3 -> 0; matrix products, arithmetic and copies ran while one was open for 19% -> 0% of each run, Pallas kernels for 0% -> 0%
where the time goes in v1:
time: 91.1 us; the launch traced here: 90.8 us
  Pallas kernels  81.3 us (89%)
  local copies, waits for them, and re-layouts  8.82 us (10%)
    pallas_call x1, Pallas kernels, shards(): pl.pallas_call(kernel, out_shape=(jax.ShapeDtypeStruct((256, 1024), BF),...  81.3 us
    unnamed x5, local copies, waits for them, and re-layouts  8.82 us

profile of v1, /device:TPU:1, one launch (start us, length us, event | category | flops | bytes accessed | tf_op | source)
XLA Modules:
  0.0 90.8 jit_solution(14912531173925866607)
XLA Ops:
  0.6 81.3 %shard_map.67 = (bf16[256,1024]{1,0:T(8,128)(2,1)}, bf16[1024,2048]{1,0:T(8,128)(2,1)}, bf16[1024,2048]{1,0:T(8,128)(2,1)}) custom-call(bf16[256,1024]{1,0:T(8,128)(2,1)} %attn.1, bf16[128,2048]{1,0:T(8,128)(2,1)} %gout.1, bf16[1024,2048]{1,0:T(8,128)(2,1)} %w_in.1, bf16[1024,2048]{1,0:T(8,128)(2,1)} %m_in.1), custom_call_target="tpu_custom_call" | custom-call | flops 17179869184 | bytes 17825792 | tf_op jit(solution)/shard_map/pallas_call | solution.py:337
  81.9 1.9 %copy.10 = bf16[256,1024]{1,0:T(8,128)(2,1)} copy(bf16[256,1024]{1,0:T(8,128)(2,1)} %get-tuple-element.6) | data formatting | bytes 1048576
  83.8 0.0 copy-start
  83.8 4.9 %copy.11 = bf16[1024,2048]{1,0:T(8,128)(2,1)} copy(bf16[1024,2048]{1,0:T(8,128)(2,1)} %get-tuple-element.7) | data formatting | bytes 8388608
  88.7 0.0 copy-done
  88.7 2.0 %copy.12 = bf16[1024,2048]{1,0:T(8,128)(2,1)} copy(bf16[1024,2048]{1,0:T(8,128)(2,1)S(1)} %copy-done) | data formatting | bytes 8388608
Async XLA Ops:
  83.8 4.9 %copy-start = (bf16[1024,2048]{1,0:T(8,128)(2,1)S(1)}, bf16[1024,2048]{1,0:T(8,128)(2,1)}, u32[]{:S(2)}) copy-start(bf16[1024,2048]{1,0:T(8,128)(2,1)} %get-tuple-element.8) | copy-start | bytes 12582916

commit v2 on v1

--- a/solution.py
+++ b/solution.py
@@ -17,16 +17,16 @@
     [(0, 0, 1), (0, 0, -1), (1, 0, 1), (1, 0, -1)],
     [(0, 1, 1), (0, 1, -1), (1, 1, 1), (1, 1, -1)],
     [(0, 2, 1), (0, 2, -1), (1, 2, 1), (1, 2, -1)],
-    [(0, -1, 1), (0, -1, -1), (1, -1, 1), (1, -1, -1)],
-    [(0, 0, 2), (0, 2, 2), (1, 0, 2), (1, 2, 2)],
-    [(0, 1, 2), (0, -1, 2), (1, 1, 2), (1, -1, 2)],
+    [(0, -1, 1), (0, -1, -1), (1, 0, 2), (0, 1, 2)],
+    [(1, -1, 1), (1, -1, -1), (1, 1, 2), (0, 2, 2)],
+    [(0, -1, 2), (1, 2, 2), (0, 0, 2), (1, -1, 2)],
 ]
 SLOT = {piece: (g, j) for g, group in enumerate(GROUPS) for j, piece in enumerate(group)}
 DU = (0, 1, 2, -1)
 
 
 def kernel(attn, gout, w_in, m_in, gin_o, nw_o, nm_o,
-           G, A, W, M, acc, AG, part, sib, mid, fin,
+           G, A, acc, AG, part, sib, mid, fin,
            ag_s, ag_r, at_s, at_r, x_s, x_r, y_s, mid_r, fin_r, loc):
     r = lax.axis_index("row")
     c = lax.axis_index("col")
@@ -54,8 +54,8 @@
         pltpu.make_async_copy(gout.at[pl.ds(0, 64), :], slot((0, 0, 0)), loc.at[0]),
         pltpu.make_async_copy(gout.at[pl.ds(64, 64), :], slot((1, 0, 0)), loc.at[1]),
         pltpu.make_async_copy(attn, A.at[pl.ds(c * 256, 256), :], loc.at[2]),
-        pltpu.make_async_copy(w_in, W, loc.at[3]),
-        pltpu.make_async_copy(m_in, M, loc.at[4]),
+        pltpu.make_async_copy(w_in, nw_o, loc.at[3]),
+        pltpu.make_async_copy(m_in, nm_o, loc.at[4]),
     ]
     for copy in locals_:
         copy.start()
@@ -75,13 +75,13 @@
     ag = {key: remote(src, dst, ag_s.at[i], ag_r.at[i], dev)
           for i, (key, (src, dst, dev)) in enumerate(ag.items())}
 
-    def send(kind, *rest):
-        for h in (0, 1):
+    def send(kind, *rest, half=(0, 1)):
+        for h in half:
             for s in (1, -1):
                 ag[(kind, h, *rest, s)].start()
 
-    def recv(kind, *rest):
-        for h in (0, 1):
+    def recv(kind, *rest, half=(0, 1)):
+        for h in half:
             for s in (1, -1):
                 ag[(kind, h, *rest, s)].wait_recv()
 
@@ -93,7 +93,11 @@
         return remote(src, dst, at_s.at[i], at_r.at[i], dev)
 
     up, down, other = at(dy=1), at(dy=-1), at(dk=1)
-    a_own = {1: attn_copy(0, attn, block(0), up), -1: attn_copy(1, attn, block(0), down)}
+    def a_half(i, lo, dev):
+        return attn_copy(i, attn.at[pl.ds(lo, 128), :], block(0, 0, lo, 128), dev)
+
+    a_own = {1: (a_half(0, 0, up), a_half(9, 128, up)),
+             -1: (a_half(1, 128, down), a_half(10, 0, down))}
     a_sib = attn_copy(2, attn, block(0), other)
     a_fwd = {1: attn_copy(3, block(-1, 0, 0, 128), block(-1, 0, 0, 128), up),
              -1: attn_copy(4, block(1, 0, 128, 128), block(1, 0, 128, 128), down)}
@@ -129,16 +133,16 @@
         dev = {"row": r, "col": ((y + 1 + 2 * q) % 4) * 2 + k}
         return remote(rows(g, j), fin.at[o, q], y_s.at[p, 0], fin_r.at[o, q], dev)
 
-    def step1(g):
-        for j in range(4):
+    def step1(g, js=(0, 1, 2, 3)):
+        for j in js:
             _, _, _, mine, _ = place(g, j)
 
             @pl.when(jnp.logical_not(mine))
             def _():
                 to_sibling(g, j).start()
 
-    def step2(g):
-        for j in range(4):
+    def step2(g, js=(0, 1, 2, 3)):
+        for j in js:
             p, _, d, mine, _ = place(g, j)
 
             @pl.when(mine)
@@ -152,8 +156,8 @@
                     to_mid(g, j, 0).start()
                     to_mid(g, j, 1).start()
 
-    def step3(g):
-        for j in range(4):
+    def step3(g, js=(0, 1, 2, 3)):
+        for j in js:
             p, _, d, mine, _ = place(g, j)
 
             @pl.when(jnp.logical_and(mine, d % 2 == 1))
@@ -165,8 +169,8 @@
                     part[g, pl.ds(64 * j, 64), f].astype(F32) + mid[p].astype(F32)).astype(BF)
                 to_owner(g, j).start()
 
-    def step4(g):
-        for j in range(4):
+    def step4(g, js=(0, 1, 2, 3)):
+        for j in js:
             _, _, d, mine, o = place(g, j)
 
             @pl.when(jnp.logical_and(mine, d == 0))
@@ -194,11 +198,11 @@
             def _():
                 to_owner(g, j).wait_send()
 
-    def partial(g):
+    def partial(g, lo=0, n_rows=256):
         def tile(n, _):
             n = pl.multiple_of(n * 512, 512)
-            part[g, :, pl.ds(n, 512)] = lax.dot_general(
-                G[g // 2, pl.ds((g % 2) * 256, 256), :], W[pl.ds(n, 512), :], NT,
+            part[g, pl.ds(lo, n_rows), pl.ds(n, 512)] = lax.dot_general(
+                G[g // 2, pl.ds((g % 2) * 256 + lo, n_rows), :], nw_o[pl.ds(n, 512), :], NT,
                 preferred_element_type=F32).astype(BF)
             return 0
 
@@ -209,9 +213,10 @@
             _, token, _, _, _ = place(g, j)
             AG[pl.ds((g % 2) * 256 + 64 * j, 64), :] = A[pl.ds(pl.multiple_of(token, 64), 64), :]
 
-    def grad_w(p, first, last):
-        collect(2 * p)
-        collect(2 * p + 1)
+    def grad_w(p, first, last, tiles=(0, 4)):
+        if tiles[0] == 0:
+            collect(2 * p)
+            collect(2 * p + 1)
 
         def tile(i, _):
             f = pl.ds(pl.multiple_of(i * 256, 256), 256)
@@ -219,14 +224,14 @@
             if not first:
                 t = acc[f, :] + t
             if last:
-                mom = 0.9 * M[f, :].astype(F32) + t
+                mom = 0.9 * nm_o[f, :].astype(F32) + t
                 nm_o[f, :] = mom.astype(BF)
-                nw_o[f, :] = (W[f, :].astype(F32) - 0.25 * mom).astype(BF)
+                nw_o[f, :] = (nw_o[f, :].astype(F32) - 0.25 * mom).astype(BF)
             else:
                 acc[f, :] = t
             return 0
 
-        lax.fori_loop(0, 4, tile, 0)
+        lax.fori_loop(*tiles, tile, 0)
 
     barrier = pltpu.get_barrier_semaphore()
     neighbours = [at(dx=1), at(dx=-1), at(dz=1), at(dz=-1), up, down, other]
@@ -235,132 +240,167 @@
     pl.semaphore_wait(barrier, len(neighbours))
 
     send("P")
-    for s in (1, -1):
-        a_own[s].start()
+    for i in (0, 1):
+        for s in (1, -1):
+            a_own[s][i].start()
     a_sib.start()
     send("S", 0)
 
     recv("P")
     send("PF")
     send("S", 1)
+    for s in (1, -1):
+        a_own[s][0].wait_recv()
+        a_fwd[s].start()
     for copy in locals_[:4]:
         copy.wait()
-
     recv("S", 0)
     for s in (1, -1):
-        a_own[s].wait_recv()
-        a_fwd[s].start()
-    for s in (1, -1):
+        a_own[s][1].wait_recv()
         a_pass[s].start()
     partial(2)
+    step1(2)
     recv("PF")
     send("S", 2)
+    send("F", 0, half=(1,))
     send("S", -1)
-    send("F", 0)
-    step1(2)
     partial(0)
     step1(0)
     step2(2)
+    for s in (1, -1):
+        a_fwd[s].wait_recv()
+        a_last[s].start()
     partial(1)
     step1(1)
     step2(0)
+    a_sib.wait_recv()
+    for s in (1, -1):
+        a_pass[s].wait_recv()
+    for s in (1, -1):
+        a_last[s].wait_recv()
+    grad_w(0, True, False, (0, 2))
     step3(2)
-    a_sib.wait_recv()
-    for s in (1, -1):
-        a_fwd[s].wait_recv()
-        a_last[s].start()
-    for s in (1, -1):
-        a_pass[s].wait_recv()
-    step2(1)
-    for s in (1, -1):
-        a_last[s].wait_recv()
-    grad_w(0, True, False)
-    step3(0)
-    step3(1)
+    step2(1, (0, 1))
     recv("S", 1)
+    send("F", 1)
     partial(3)
     step1(3)
-    step4(2)
-    grad_w(1, False, False)
+    grad_w(0, True, False, (2, 4))
+    step2(1, (2, 3))
+    step3(0)
+    grad_w(1, False, False, (0, 2))
     step2(3)
-    step4(0)
-    step4(1)
+    grad_w(1, False, False, (2, 4))
+    step3(1, (0,))
     recv("S", 2)
     send("F", 2)
-    send("F", 1)
     partial(4)
     step1(4)
+    step3(1, (1,))
+    step2(4)
     step3(3)
-    recv("S", -1)
-    send("F", -1)
-    step2(4)
+    recv("S", -1, half=(0,))
+    send("F", -1, half=(0,))
+    send("F", 0, half=(0,))
+    step3(1, (2,))
+    recv("S", -1, half=(1,))
+    send("F", -1, half=(1,))
+    recv("F", 1, half=(0,))
+    recv("F", 0, half=(1,))
     partial(5)
     step1(5)
     step3(4)
-    step4(3)
-    grad_w(2, False, False)
+    grad_w(2, False, False, (0, 2))
     step2(5)
-    step4(4)
-    recv("F", 0)
-    recv("F", 2)
+    recv("F", 2, half=(0,))
+    recv("F", 1, half=(1,))
     partial(6)
     step1(6)
+    step3(1, (3,))
+    grad_w(2, False, False, (2, 4))
+    step2(6)
     step3(5)
-    step4(5)
-    step2(6)
-    recv("F", 1)
-    recv("F", -1)
-    partial(7)
-    step1(7)
+    recv("F", -1, half=(0,))
+    recv("F", 2, half=(1,))
+    partial(7, 0, 128)
+    step1(7, (0, 1))
+    for g in (2, 0, 1, 3, 4):
+        step4(g)
+    recv("F", 0, half=(0,))
+    recv("F", -1, half=(1,))
+    partial(7, 128, 128)
+    step1(7, (2, 3))
+    step2(7, (0, 1))
     step3(6)
-    step2(7)
-    step4(6)
     locals_[4].wait()
-    step3(7)
-    grad_w(3, False, True)
-    step4(7)
+    grad_w(3, False, True, (0, 2))
+    step2(7, (2, 3))
+    step3(7, (0, 1))
+    grad_w(3, False, True, (2, 4))
+    step3(7, (2, 3))
+    for g in (5, 6, 7):
+        step4(g)
 
     for copy in ag.values():
         copy.wait_send()
-    for copies in (a_own, a_fwd, a_pass, a_last):
-        for s in (1, -1):
-            copies[s].wait_send()
+    for s in (1, -1):
+        for copy in (*a_own[s], a_fwd[s], a_pass[s], a_last[s]):
+            copy.wait_send()
     a_sib.wait_send()
     for g in range(8):
         drain(g)
+
+
+def store(gin, nw, nm, gin_o, nw_o, nm_o, sem):
+    copies = [pltpu.make_async_copy(nw, nw_o, sem.at[0]), pltpu.make_async_copy(nm, nm_o, sem.at[1]),
+              pltpu.make_async_copy(gin, gin_o, sem.at[2])]
+    for copy in copies:
+        copy.start()
+    for copy in copies:
+        copy.wait()
 
 
 def shards(attn, grad_out, weight, momentum):
     hbm = pl.BlockSpec(memory_space=pl.ANY)
     vmem = pl.BlockSpec(memory_space=pltpu.VMEM)
     dma = pltpu.SemaphoreType.DMA
-    return pl.pallas_call(
+    results = pl.pallas_call(
         kernel,
         out_shape=(
-            jax.ShapeDtypeStruct((256, 1024), BF),
-            jax.ShapeDtypeStruct((1024, 2048), BF),
-            jax.ShapeDtypeStruct((1024, 2048), BF),
+            pltpu.VMEM((256, 1024), BF),
+            pltpu.VMEM((1024, 2048), BF),
+            pltpu.VMEM((1024, 2048), BF),
         ),
         in_specs=[hbm] * 4,
         out_specs=(vmem,) * 3,
         scratch_shapes=[
             pltpu.VMEM((4, 512, 2048), BF),
             pltpu.VMEM((2048, 1024), BF),
-            pltpu.VMEM((1024, 2048), BF),
-            pltpu.VMEM((1024, 2048), BF),
             pltpu.VMEM((1024, 2048), F32),
             pltpu.VMEM((512, 1024), BF),
             pltpu.VMEM((8, 256, 1024), BF),
             pltpu.VMEM((32, 64, 1024), BF),
             pltpu.VMEM((32, 64, 512), BF),
             pltpu.VMEM((4, 2, 64, 1024), BF),
-            dma((40,)), dma((40,)), dma((9,)), dma((9,)),
+            dma((40,)), dma((40,)), dma((11,)), dma((11,)),
             dma((32,)), dma((32,)), dma((32, 2)), dma((32,)), dma((4, 2)), dma((5,)),
         ],
         compiler_params=pltpu.CompilerParams(
-            collective_id=0, has_side_effects=True, vmem_limit_bytes=67043328),
+            collective_id=0, has_side_effects=True, vmem_limit_bytes=52428800),
         cost_estimate=pl.CostEstimate(flops=4 * 2048 * 1024 * 2048, bytes_accessed=17 << 20, transcendentals=0),
     )(attn, grad_out, weight, momentum)
+    return pl.pallas_call(
+        store,
+        out_shape=(
+            jax.ShapeDtypeStruct((256, 1024), BF),
+            jax.ShapeDtypeStruct((1024, 2048), BF),
+            jax.ShapeDtypeStruct((1024, 2048), BF),
+        ),
+        in_specs=[vmem] * 3,
+        out_specs=(hbm,) * 3,
+        scratch_shapes=[dma((3,))],
+        compiler_params=pltpu.CompilerParams(vmem_limit_bytes=1 << 20),
+    )(*[pltpu.with_memory_space_constraint(r, pltpu.VMEM) for r in results])
 
 
 def solution(mesh):

time: 91.1 us -> 70.9 us (0.78)
  Pallas kernels: 81.3 us -> 69.9 us
  local copies, waits for them, and re-layouts: 8.82 us -> 0 us
    pallas_call x1 -> x2, Pallas kernels: 81.3 us -> 69.9 us  [the longest x1 66.5 us: shards(): pl.pallas_call(kernel, out_shape=(pltpu.VMEM((256, 1024), BF), pltpu.VMEM...]
    unnamed x5 -> x0, local copies, waits for them, and re-layouts: 8.82 us -> none
where the time goes in v2:
time: 70.9 us; the launch traced here: 70.7 us
  Pallas kernels  69.9 us (99%)
  between operations  0.8 us (1%)
    pallas_call x1, Pallas kernels, shards(): pl.pallas_call(kernel, out_shape=(pltpu.VMEM((256, 1024), BF), pltpu.VMEM...  66.5 us
    pallas_call x1, Pallas kernels, shards(): pl.pallas_call(store, out_shape=(jax.ShapeDtypeStruct((256, 1024), BF), j...  3.46 us

profile of v2, /device:TPU:1, one launch (start us, length us, event | category | flops | bytes accessed | tf_op | source)
XLA Modules:
  0.0 70.7 jit_solution(11744633847110906266)
XLA Ops:
  0.6 66.5 %shard_map.67 = (bf16[256,1024]{1,0:T(8,128)(2,1)S(1)}, bf16[1024,2048]{1,0:T(8,128)(2,1)S(1)}, bf16[1024,2048]{1,0:T(8,128)(2,1)S(1)}) custom-call(bf16[256,1024]{1,0:T(8,128)(2,1)} %attn.1, bf16[128,2048]{1,0:T(8,128)(2,1)} %gout.1, bf16[1024,2048]{1,0:T(8,128)(2,1)} %w_in.1, bf16[1024,2048]{1,0:T(8,128)(2,1)} %m_in.1), custom_call_target="tpu_custom_call" | custom-call | flops 17179869184 | bytes 17825792 | tf_op jit(solution)/shard_map/pallas_call | solution.py:367
  67.1 3.5 %shard_map.68 = (bf16[256,1024]{1,0:T(8,128)(2,1)}, bf16[1024,2048]{1,0:T(8,128)(2,1)}, bf16[1024,2048]{1,0:T(8,128)(2,1)}) custom-call(bf16[256,1024]{1,0:T(8,128)(2,1)S(1)} %get-tuple-element.6.gin, bf16[1024,2048]{1,0:T(8,128)(2,1)S(1)} %get-tuple-element.7.nw, bf16[1024,2048]{1,0:T(8,128)(2,1)S(1)} %get-tuple-element.8.nm), custom_call_target="tpu_custom_call" | custom-call | tf_op jit(solution)/shard_map/pallas_call | solution.py:392

commit v3 on v2

--- a/solution.py
+++ b/solution.py
@@ -43,7 +43,7 @@
 
     def slot(piece, lo=0, n=64):
         g, j = SLOT[piece]
-        return G.at[g // 2, pl.ds((g % 2) * 256 + j * 64 + lo, n), :]
+        return G.at[pl.ds(g * 256 + j * 64 + lo, n), :]
 
     def remote(src, dst, ss, rs, dev):
         return pltpu.make_async_remote_copy(
@@ -59,6 +59,8 @@
     ]
     for copy in locals_:
         copy.start()
+
+    up, down, other = at(dy=1), at(dy=-1), at(dk=1)
 
     ag = {}
     for h in (0, 1):
@@ -72,8 +74,12 @@
                 src = own if du == 0 else slot((h, du, 0))
                 ag["S", h, du, s] = (src, slot((h, du, -s)), along(h, False, s))
                 ag["F", h, du, s] = (slot((h, du, -s), q, 32), slot((h, du, 2), q, 32), along(h, False, s))
-    ag = {key: remote(src, dst, ag_s.at[i], ag_r.at[i], dev)
-          for i, (key, (src, dst, dev)) in enumerate(ag.items())}
+    waits = []
+    for key in ag:
+        if key[:-1] not in waits:
+            waits.append(key[:-1])
+    ag = {key: remote(src, dst, ag_s.at[0], ag_r.at[waits.index(key[:-1])], dev)
+          for key, (src, dst, dev) in ag.items()}
 
     def send(kind, *rest, half=(0, 1)):
         for h in half:
@@ -82,17 +88,22 @@
 
     def recv(kind, *rest, half=(0, 1)):
         for h in half:
-            for s in (1, -1):
-                ag[(kind, h, *rest, s)].wait_recv()
+            if kind == "P":
+                landed = slot((h, 1, 0), 0, 128)
+            elif kind == "S":
+                landed = slot((h, *rest, 1), 0, 128)
+            else:
+                landed = slot((h, 2, 0) if kind == "PF" else (h, *rest, 2))
+            sem = ag_r.at[waits.index((kind, h, *rest))]
+            remote(landed, landed, ag_s.at[0], sem, other).wait_recv()
 
     def block(dy, dk=0, lo=0, n=256):
         col = ((y + dy + 4) % 4) * 2 + (k + dk) % 2
         return A.at[pl.ds(pl.multiple_of(col * 256 + lo, 128), n), :]
 
     def attn_copy(i, src, dst, dev):
-        return remote(src, dst, at_s.at[i], at_r.at[i], dev)
-
-    up, down, other = at(dy=1), at(dy=-1), at(dk=1)
+        return remote(src, dst, at_s.at[0], at_r.at[i], dev)
+
     def a_half(i, lo, dev):
         return attn_copy(i, attn.at[pl.ds(lo, 128), :], block(0, 0, lo, 128), dev)
 
@@ -113,25 +124,27 @@
         d = (xs - y + 4) % 4
         mine = zs // 2 == k
         o = (zs % 2) * 2 + h
-        return 4 * g + j, xs * 512 + zs * 128 + 64 * h, d, mine, o
+        return (dx + 4) % 4 * 4 + o, xs * 512 + zs * 128 + 64 * h, d, mine, o
 
     def rows(g, j):
         return part.at[g, pl.ds(64 * j, 64), :]
 
     def to_sibling(g, j):
-        p = 4 * g + j
-        return remote(rows(g, j), sib.at[p], x_s.at[p], x_r.at[p], other)
+        p = place(g, j)[0]
+        return remote(rows(g, j), sib.at[p], x_s.at[0], x_r.at[p], other)
 
     def to_mid(g, j, q):
-        p = 4 * g + j
-        return remote(part.at[g, pl.ds(64 * j, 64), pl.ds(512 * q, 512)], mid.at[p],
-                      y_s.at[p, q], mid_r.at[p], up if q == 0 else down)
-
-    def to_owner(g, j):
-        p, _, d, _, o = place(g, j)
+        n = 4 * q + place(g, j)[4]
+        return remote(part.at[g, pl.ds(64 * j, 64), pl.ds(512 * q, 512)], mid.at[n],
+                      y_s.at[0], mid_r.at[n], up if q == 0 else down)
+
+    def to_owner(g, j, late):
+        _, _, d, _, o = place(g, j)
         q = (d == 3).astype(jnp.int32)
+        f = pl.ds(pl.multiple_of((q if late else 1 - q) * 512, 512), 512)
         dev = {"row": r, "col": ((y + 1 + 2 * q) % 4) * 2 + k}
-        return remote(rows(g, j), fin.at[o, q], y_s.at[p, 0], fin_r.at[o, q], dev)
+        return remote(part.at[g, pl.ds(64 * j, 64), f], fin.at[o, q, :, f],
+                      y_s.at[0], fin_r.at[o, q], dev)
 
     def step1(g, js=(0, 1, 2, 3)):
         for j in js:
@@ -156,18 +169,23 @@
                     to_mid(g, j, 0).start()
                     to_mid(g, j, 1).start()
 
+                @pl.when(d % 2 == 1)
+                def _():
+                    to_owner(g, j, 0).start()
+
     def step3(g, js=(0, 1, 2, 3)):
         for j in js:
-            p, _, d, mine, _ = place(g, j)
+            _, _, d, mine, o = place(g, j)
 
             @pl.when(jnp.logical_and(mine, d % 2 == 1))
             def _():
                 q = (d == 3).astype(jnp.int32)
-                to_mid(g, j, 0).wait_recv()
+                n = 4 * q + o
+                remote(mid.at[n], mid.at[n], y_s.at[0], mid_r.at[n], up).wait_recv()
                 f = pl.ds(pl.multiple_of(q * 512, 512), 512)
                 part[g, pl.ds(64 * j, 64), f] = (
-                    part[g, pl.ds(64 * j, 64), f].astype(F32) + mid[p].astype(F32)).astype(BF)
-                to_owner(g, j).start()
+                    part[g, pl.ds(64 * j, 64), f].astype(F32) + mid[n].astype(F32)).astype(BF)
+                to_owner(g, j, 1).start()
 
     def step4(g, js=(0, 1, 2, 3)):
         for j in js:
@@ -176,54 +194,42 @@
             @pl.when(jnp.logical_and(mine, d == 0))
             def _():
                 for q in (0, 1):
-                    remote(rows(g, j), fin.at[o, q], y_s.at[4 * g + j, 0], fin_r.at[o, q], up).wait_recv()
+                    remote(fin.at[o, q], fin.at[o, q], y_s.at[0], fin_r.at[o, q], up).wait_recv()
                 gin_o[pl.ds(pl.multiple_of(o * 64, 64), 64), :] = (
                     part[g, pl.ds(64 * j, 64), :].astype(F32)
                     + fin[o, 0].astype(F32) + fin[o, 1].astype(F32)).astype(BF)
 
-    def drain(g):
-        for j in range(4):
-            _, _, d, mine, _ = place(g, j)
-
-            @pl.when(jnp.logical_not(mine))
-            def _():
-                to_sibling(g, j).wait_send()
-
-            @pl.when(jnp.logical_and(mine, d == 2))
-            def _():
-                to_mid(g, j, 0).wait_send()
-                to_mid(g, j, 1).wait_send()
-
-            @pl.when(jnp.logical_and(mine, d % 2 == 1))
-            def _():
-                to_owner(g, j).wait_send()
+    def sent(ref, sem):
+        remote(ref, ref, sem, x_r.at[0], other).wait_send()
 
     def partial(g, lo=0, n_rows=256):
         def tile(n, _):
             n = pl.multiple_of(n * 512, 512)
             part[g, pl.ds(lo, n_rows), pl.ds(n, 512)] = lax.dot_general(
-                G[g // 2, pl.ds((g % 2) * 256 + lo, n_rows), :], nw_o[pl.ds(n, 512), :], NT,
+                G[pl.ds(g * 256 + lo, n_rows), :], nw_o[pl.ds(n, 512), :], NT,
                 preferred_element_type=F32).astype(BF)
             return 0
 
         lax.fori_loop(0, 2, tile, 0)
 
-    def collect(g):
-        for j in range(4):
-            _, token, _, _, _ = place(g, j)
-            AG[pl.ds((g % 2) * 256 + 64 * j, 64), :] = A[pl.ds(pl.multiple_of(token, 64), 64), :]
-
-    def grad_w(p, first, last, tiles=(0, 4)):
-        if tiles[0] == 0:
-            collect(2 * p)
-            collect(2 * p + 1)
+    def collect(groups):
+        for i, g in enumerate(groups):
+            for j in range(4):
+                _, token, _, _, _ = place(g, j)
+                AG[pl.ds(256 * i + 64 * j, 64), :] = A[pl.ds(pl.multiple_of(token, 64), 64), :]
+
+    def grad_w(groups, lo, hi):
+        n = 256 * len(groups)
+        tokens = pl.ds(256 * groups[0], n)
+        if lo == 0:
+            collect(groups)
 
         def tile(i, _):
             f = pl.ds(pl.multiple_of(i * 256, 256), 256)
-            t = lax.dot_general(AG[:, f], G[p], TN, preferred_element_type=F32)
-            if not first:
+            t = lax.dot_general(AG[pl.ds(0, n), f], G[tokens, :], TN, preferred_element_type=F32)
+            if groups[0] > 0:
                 t = acc[f, :] + t
-            if last:
+            if groups[-1] == 7:
                 mom = 0.9 * nm_o[f, :].astype(F32) + t
                 nm_o[f, :] = mom.astype(BF)
                 nw_o[f, :] = (nw_o[f, :].astype(F32) - 0.25 * mom).astype(BF)
@@ -231,7 +237,7 @@
                 acc[f, :] = t
             return 0
 
-        lax.fori_loop(*tiles, tile, 0)
+        lax.fori_loop(lo, hi, tile, 0)
 
     barrier = pltpu.get_barrier_semaphore()
     neighbours = [at(dx=1), at(dx=-1), at(dz=1), at(dz=-1), up, down, other]
@@ -278,31 +284,32 @@
         a_pass[s].wait_recv()
     for s in (1, -1):
         a_last[s].wait_recv()
-    grad_w(0, True, False, (0, 2))
+    grad_w((0, 1), 0, 2)
     step3(2)
     step2(1, (0, 1))
     recv("S", 1)
     send("F", 1)
     partial(3)
     step1(3)
-    grad_w(0, True, False, (2, 4))
+    grad_w((0, 1), 2, 4)
     step2(1, (2, 3))
     step3(0)
-    grad_w(1, False, False, (0, 2))
     step2(3)
-    grad_w(1, False, False, (2, 4))
-    step3(1, (0,))
     recv("S", 2)
     send("F", 2)
     partial(4)
     step1(4)
+    step3(1, (0,))
+    grad_w((2, 3, 4), 0, 1)
     step3(1, (1,))
     step2(4)
     step3(3)
+    grad_w((2, 3, 4), 1, 3)
     recv("S", -1, half=(0,))
     send("F", -1, half=(0,))
     send("F", 0, half=(0,))
     step3(1, (2,))
+    grad_w((2, 3, 4), 3, 4)
     recv("S", -1, half=(1,))
     send("F", -1, half=(1,))
     recv("F", 1, half=(0,))
@@ -310,50 +317,49 @@
     partial(5)
     step1(5)
     step3(4)
-    grad_w(2, False, False, (0, 2))
-    step2(5)
+    step3(1, (3,))
     recv("F", 2, half=(0,))
     recv("F", 1, half=(1,))
     partial(6)
     step1(6)
-    step3(1, (3,))
-    grad_w(2, False, False, (2, 4))
-    step2(6)
-    step3(5)
+    step2(5)
+    for g in (2, 0):
+        step4(g)
     recv("F", -1, half=(0,))
     recv("F", 2, half=(1,))
     partial(7, 0, 128)
     step1(7, (0, 1))
-    for g in (2, 0, 1, 3, 4):
-        step4(g)
+    step2(6)
+    step3(5)
     recv("F", 0, half=(0,))
     recv("F", -1, half=(1,))
     partial(7, 128, 128)
     step1(7, (2, 3))
     step2(7, (0, 1))
+    locals_[4].wait()
+    grad_w((5, 6, 7), 0, 1)
+    step2(7, (2, 3))
     step3(6)
-    locals_[4].wait()
-    grad_w(3, False, True, (0, 2))
-    step2(7, (2, 3))
+    grad_w((5, 6, 7), 1, 2)
     step3(7, (0, 1))
-    grad_w(3, False, True, (2, 4))
+    grad_w((5, 6, 7), 2, 3)
     step3(7, (2, 3))
-    for g in (5, 6, 7):
+    grad_w((5, 6, 7), 3, 4)
+    sent(G.at[pl.ds(0, 1920), :], ag_s.at[0])
+    sent(A.at[pl.ds(0, 1792), :], at_s.at[0])
+    sent(sib, x_s.at[0])
+    for g in (1, 3, 4, 5, 6, 7):
         step4(g)
-
-    for copy in ag.values():
-        copy.wait_send()
-    for s in (1, -1):
-        for copy in (*a_own[s], a_fwd[s], a_pass[s], a_last[s]):
-            copy.wait_send()
-    a_sib.wait_send()
-    for g in range(8):
-        drain(g)
+    sent(sib.at[pl.ds(0, 12)], y_s.at[0])
 
 
 def store(gin, nw, nm, gin_o, nw_o, nm_o, sem):
-    copies = [pltpu.make_async_copy(nw, nw_o, sem.at[0]), pltpu.make_async_copy(nm, nm_o, sem.at[1]),
-              pltpu.make_async_copy(gin, gin_o, sem.at[2])]
+    copies = []
+    for src, dst, n in ((nw, nw_o, 8), (nm, nm_o, 8), (gin, gin_o, 1)):
+        step = src.shape[0] // n
+        for i in range(n):
+            f = pl.ds(i * step, step)
+            copies.append(pltpu.make_async_copy(src.at[f, :], dst.at[f, :], sem.at[len(copies)]))
     for copy in copies:
         copy.start()
     for copy in copies:
@@ -374,16 +380,16 @@
         in_specs=[hbm] * 4,
         out_specs=(vmem,) * 3,
         scratch_shapes=[
-            pltpu.VMEM((4, 512, 2048), BF),
+            pltpu.VMEM((2048, 2048), BF),
             pltpu.VMEM((2048, 1024), BF),
             pltpu.VMEM((1024, 2048), F32),
-            pltpu.VMEM((512, 1024), BF),
+            pltpu.VMEM((768, 1024), BF),
             pltpu.VMEM((8, 256, 1024), BF),
-            pltpu.VMEM((32, 64, 1024), BF),
-            pltpu.VMEM((32, 64, 512), BF),
+            pltpu.VMEM((16, 64, 1024), BF),
+            pltpu.VMEM((8, 64, 512), BF),
             pltpu.VMEM((4, 2, 64, 1024), BF),
-            dma((40,)), dma((40,)), dma((11,)), dma((11,)),
-            dma((32,)), dma((32,)), dma((32, 2)), dma((32,)), dma((4, 2)), dma((5,)),
+            dma((1,)), dma((20,)), dma((1,)), dma((11,)),
+            dma((1,)), dma((16,)), dma((1,)), dma((8,)), dma((4, 2)), dma((5,)),
         ],
         compiler_params=pltpu.CompilerParams(
             collective_id=0, has_side_effects=True, vmem_limit_bytes=52428800),
@@ -398,7 +404,7 @@
         ),
         in_specs=[vmem] * 3,
         out_specs=(hbm,) * 3,
-        scratch_shapes=[dma((3,))],
+        scratch_shapes=[dma((17,))],
         compiler_params=pltpu.CompilerParams(vmem_limit_bytes=1 << 20),
     )(*[pltpu.with_memory_space_constraint(r, pltpu.VMEM) for r in results])
 

time: 70.9 us -> 67.2 us (0.948)
  Pallas kernels: 69.9 us -> 66.3 us
    pallas_call x1, Pallas kernels: 66.5 us -> 62.7 us  [shards(): pl.pallas_call(kernel, out_shape=(pltpu.VMEM((256, 1024), BF), pltpu.VMEM...]
where the time goes in v3:
time: 67.2 us; the launch traced here: 67.1 us
  Pallas kernels  66.3 us (99%)
  between operations  0.8 us (1%)
    pallas_call x1, Pallas kernels, shards(): pl.pallas_call(kernel, out_shape=(pltpu.VMEM((256, 1024), BF), pltpu.VMEM...  62.7 us
    pallas_call x1, Pallas kernels, shards(): pl.pallas_call(store, out_shape=(jax.ShapeDtypeStruct((256, 1024), BF), j...  3.58 us

profile of v3, /device:TPU:1, one launch (start us, length us, event | category | flops | bytes accessed | tf_op | source)
XLA Modules:
  0.0 67.1 jit_solution(5410126923796246746)
XLA Ops:
  0.6 62.7 %shard_map.67 = (bf16[256,1024]{1,0:T(8,128)(2,1)S(1)}, bf16[1024,2048]{1,0:T(8,128)(2,1)S(1)}, bf16[1024,2048]{1,0:T(8,128)(2,1)S(1)}) custom-call(bf16[256,1024]{1,0:T(8,128)(2,1)} %attn.1, bf16[128,2048]{1,0:T(8,128)(2,1)} %gout.1, bf16[1024,2048]{1,0:T(8,128)(2,1)} %w_in.1, bf16[1024,2048]{1,0:T(8,128)(2,1)} %m_in.1), custom_call_target="tpu_custom_call" | custom-call | flops 17179869184 | bytes 17825792 | tf_op jit(solution)/shard_map/pallas_call | solution.py:373
  63.3 3.6 %shard_map.68 = (bf16[256,1024]{1,0:T(8,128)(2,1)}, bf16[1024,2048]{1,0:T(8,128)(2,1)}, bf16[1024,2048]{1,0:T(8,128)(2,1)}) custom-call(bf16[256,1024]{1,0:T(8,128)(2,1)S(1)} %get-tuple-element.6.gin, bf16[1024,2048]{1,0:T(8,128)(2,1)S(1)} %get-tuple-element.7.nw, bf16[1024,2048]{1,0:T(8,128)(2,1)S(1)} %get-tuple-element.8.nm), custom_call_target="tpu_custom_call" | custom-call | tf_op jit(solution)/shard_map/pallas_call | solution.py:398

commit v4 on v3

--- a/solution.py
+++ b/solution.py
@@ -23,6 +23,7 @@
 ]
 SLOT = {piece: (g, j) for g, group in enumerate(GROUPS) for j, piece in enumerate(group)}
 DU = (0, 1, 2, -1)
+DIRECT = ((7, 2), (7, 3))
 
 
 def kernel(attn, gout, w_in, m_in, gin_o, nw_o, nm_o,
@@ -154,9 +155,11 @@
             def _():
                 to_sibling(g, j).start()
 
-    def step2(g, js=(0, 1, 2, 3)):
+    def step2(g, js=(0, 1, 2, 3), core=None):
         for j in js:
             p, _, d, mine, _ = place(g, j)
+            if core is not None:
+                mine = jnp.logical_and(mine, k == core)
 
             @pl.when(mine)
             def _():
@@ -169,13 +172,39 @@
                     to_mid(g, j, 0).start()
                     to_mid(g, j, 1).start()
 
-                @pl.when(d % 2 == 1)
+        early(g, js, core)
+
+    def direct(g, js, core):
+        for j in js:
+            p, _, d, mine, o = place(g, j)
+
+            @pl.when(jnp.logical_and(mine, k == core))
+            def _():
+                to_sibling(g, j).wait_recv()
+                part[g, pl.ds(64 * j, 64), :] = (
+                    part[g, pl.ds(64 * j, 64), :].astype(F32) + sib[p].astype(F32)).astype(BF)
+
+                @pl.when(d > 0)
                 def _():
-                    to_owner(g, j, 0).start()
-
-    def step3(g, js=(0, 1, 2, 3)):
+                    q = 2 * (d == 2).astype(jnp.int32) + (d == 3).astype(jnp.int32)
+                    dev = {"row": r, "col": ((y + d) % 4) * 2 + k}
+                    remote(rows(g, j), fin.at[o, q], y_s.at[0], fin_r.at[o, q], dev).start()
+
+    def early(g, js, core):
+        for j in js:
+            _, _, d, mine, _ = place(g, j)
+            if core is not None:
+                mine = jnp.logical_and(mine, k == core)
+
+            @pl.when(jnp.logical_and(mine, d % 2 == 1))
+            def _():
+                to_owner(g, j, 0).start()
+
+    def step3(g, js=(0, 1, 2, 3), core=None):
         for j in js:
             _, _, d, mine, o = place(g, j)
+            if core is not None:
+                mine = jnp.logical_and(mine, k == core)
 
             @pl.when(jnp.logical_and(mine, d % 2 == 1))
             def _():
@@ -193,14 +222,29 @@
 
             @pl.when(jnp.logical_and(mine, d == 0))
             def _():
-                for q in (0, 1):
+                t = part[g, pl.ds(64 * j, 64), :].astype(F32)
+                for q in range(3 if (g, j) in DIRECT else 2):
                     remote(fin.at[o, q], fin.at[o, q], y_s.at[0], fin_r.at[o, q], up).wait_recv()
-                gin_o[pl.ds(pl.multiple_of(o * 64, 64), 64), :] = (
-                    part[g, pl.ds(64 * j, 64), :].astype(F32)
-                    + fin[o, 0].astype(F32) + fin[o, 1].astype(F32)).astype(BF)
+                    t = t + fin[o, q].astype(F32)
+                gin_o[pl.ds(pl.multiple_of(o * 64, 64), 64), :] = t.astype(BF)
 
     def sent(ref, sem):
         remote(ref, ref, sem, x_r.at[0], other).wait_send()
+
+    def last_partial(g, js):
+        lo, n_rows = 64 * js[0], 64 * len(js)
+        for q in (0, 1):
+            f = pl.ds(512 * q, 512)
+            part[g, pl.ds(lo, n_rows), f] = lax.dot_general(
+                G[pl.ds(g * 256 + lo, n_rows), :], nw_o[f, :], NT,
+                preferred_element_type=F32).astype(BF)
+            for j in js:
+                p, _, _, mine, _ = place(g, j)
+
+                @pl.when(jnp.logical_not(mine))
+                def _():
+                    remote(part.at[g, pl.ds(64 * j, 64), f], sib.at[p, :, f],
+                           x_s.at[0], x_r.at[p], other).start()
 
     def partial(g, lo=0, n_rows=256):
         def tile(n, _):
@@ -330,20 +374,20 @@
     partial(7, 0, 128)
     step1(7, (0, 1))
     step2(6)
-    step3(5)
     recv("F", 0, half=(0,))
     recv("F", -1, half=(1,))
-    partial(7, 128, 128)
-    step1(7, (2, 3))
-    step2(7, (0, 1))
+    step3(5)
+    step2(7, (0, 1), 0)
+    last_partial(7, (2, 3))
+    direct(7, (2, 3), 0)
     locals_[4].wait()
     grad_w((5, 6, 7), 0, 1)
-    step2(7, (2, 3))
+    step2(7, (0, 1), 1)
     step3(6)
     grad_w((5, 6, 7), 1, 2)
+    direct(7, (2, 3), 1)
+    grad_w((5, 6, 7), 2, 3)
     step3(7, (0, 1))
-    grad_w((5, 6, 7), 2, 3)
-    step3(7, (2, 3))
     grad_w((5, 6, 7), 3, 4)
     sent(G.at[pl.ds(0, 1920), :], ag_s.at[0])
     sent(A.at[pl.ds(0, 1792), :], at_s.at[0])
@@ -387,9 +431,9 @@
             pltpu.VMEM((8, 256, 1024), BF),
             pltpu.VMEM((16, 64, 1024), BF),
             pltpu.VMEM((8, 64, 512), BF),
-            pltpu.VMEM((4, 2, 64, 1024), BF),
+            pltpu.VMEM((4, 3, 64, 1024), BF),
             dma((1,)), dma((20,)), dma((1,)), dma((11,)),
-            dma((1,)), dma((16,)), dma((1,)), dma((8,)), dma((4, 2)), dma((5,)),
+            dma((1,)), dma((16,)), dma((1,)), dma((8,)), dma((4, 3)), dma((5,)),
         ],
         compiler_params=pltpu.CompilerParams(
             collective_id=0, has_side_effects=True, vmem_limit_bytes=52428800),

time: 67.2 us -> 65.9 us (0.981)
  Pallas kernels: 66.3 us -> 64.9 us
    pallas_call x1, Pallas kernels: 62.7 us -> 61.3 us  [shards(): pl.pallas_call(kernel, out_shape=(pltpu.VMEM((256, 1024), BF), pltpu.VMEM...]
where the time goes in v4:
time: 65.9 us; the launch traced here: 65.7 us
  Pallas kernels  64.9 us (98%)
  between operations  0.8 us (1%)
    pallas_call x1, Pallas kernels, shards(): pl.pallas_call(kernel, out_shape=(pltpu.VMEM((256, 1024), BF), pltpu.VMEM...  61.3 us
    pallas_call x1, Pallas kernels, shards(): pl.pallas_call(store, out_shape=(jax.ShapeDtypeStruct((256, 1024), BF), j...  3.58 us

profile of v4, /device:TPU:1, one launch (start us, length us, event | category | flops | bytes accessed | tf_op | source)
XLA Modules:
  0.0 65.7 jit_solution(3449134479375215473)
XLA Ops:
  0.6 61.3 %shard_map.67 = (bf16[256,1024]{1,0:T(8,128)(2,1)S(1)}, bf16[1024,2048]{1,0:T(8,128)(2,1)S(1)}, bf16[1024,2048]{1,0:T(8,128)(2,1)S(1)}) custom-call(bf16[256,1024]{1,0:T(8,128)(2,1)} %attn.1, bf16[128,2048]{1,0:T(8,128)(2,1)} %gout.1, bf16[1024,2048]{1,0:T(8,128)(2,1)} %w_in.1, bf16[1024,2048]{1,0:T(8,128)(2,1)} %m_in.1), custom_call_target="tpu_custom_call" | custom-call | flops 17179869184 | bytes 17825792 | tf_op jit(solution)/shard_map/pallas_call | solution.py:417
  62.0 3.6 %shard_map.68 = (bf16[256,1024]{1,0:T(8,128)(2,1)}, bf16[1024,2048]{1,0:T(8,128)(2,1)}, bf16[1024,2048]{1,0:T(8,128)(2,1)}) custom-call(bf16[256,1024]{1,0:T(8,128)(2,1)S(1)} %get-tuple-element.6.gin, bf16[1024,2048]{1,0:T(8,128)(2,1)S(1)} %get-tuple-element.7.nw, bf16[1024,2048]{1,0:T(8,128)(2,1)S(1)} %get-tuple-element.8.nm), custom_call_target="tpu_custom_call" | custom-call | tf_op jit(solution)/shard_map/pallas_call | solution.py:442

commit v5 on v4

--- a/solution.py
+++ b/solution.py
@@ -17,8 +17,8 @@
     [(0, 0, 1), (0, 0, -1), (1, 0, 1), (1, 0, -1)],
     [(0, 1, 1), (0, 1, -1), (1, 1, 1), (1, 1, -1)],
     [(0, 2, 1), (0, 2, -1), (1, 2, 1), (1, 2, -1)],
-    [(0, -1, 1), (0, -1, -1), (1, 0, 2), (0, 1, 2)],
-    [(1, -1, 1), (1, -1, -1), (1, 1, 2), (0, 2, 2)],
+    [(0, -1, 1), (0, -1, -1), (1, 0, 2), (1, 1, 2)],
+    [(0, 1, 2), (0, 2, 2), (1, -1, 1), (1, -1, -1)],
     [(0, -1, 2), (1, 2, 2), (0, 0, 2), (1, -1, 2)],
 ]
 SLOT = {piece: (g, j) for g, group in enumerate(GROUPS) for j, piece in enumerate(group)}
@@ -28,7 +28,7 @@
 
 def kernel(attn, gout, w_in, m_in, gin_o, nw_o, nm_o,
            G, A, acc, AG, part, sib, mid, fin,
-           ag_s, ag_r, at_s, at_r, x_s, x_r, y_s, mid_r, fin_r, loc):
+           sib7, x7_s, x7_r, y7_s, ag_s, ag_r, at_s, at_r, x_s, x_r, y_s, mid_r, fin_r, loc):
     r = lax.axis_index("row")
     c = lax.axis_index("col")
     x, z, y, k = r // 4, r % 4, c // 2, c % 2
@@ -174,21 +174,37 @@
 
         early(g, js, core)
 
+    def feats(core):
+        return pl.ds(pl.multiple_of(core * 512, 512), 512)
+
+    def swap(g, j, i):
+        return remote(part.at[g, pl.ds(64 * j, 64), feats(1 - k)], sib7.at[i],
+                      x7_s.at[0], x7_r.at[i], other)
+
+    def half_to_owner(g, j, i):
+        _, _, d, mine, o = place(g, j)
+        q = jnp.where(d == 0, 3, jnp.where(d == 1, 0, jnp.where(d == 3, 1, 2)))
+        owner = jnp.where(mine, k, 1 - k)
+        dev = {"row": r, "col": ((y + d) % 4) * 2 + owner}
+        return remote(part.at[g, pl.ds(64 * j, 64), feats(k)], fin.at[o, q, :, feats(k)],
+                      y7_s.at[i], fin_r.at[o, q], dev)
+
+    def away(g, j):
+        _, _, d, mine, _ = place(g, j)
+        return jnp.logical_not(jnp.logical_and(mine, d == 0))
+
     def direct(g, js, core):
-        for j in js:
-            p, _, d, mine, o = place(g, j)
-
-            @pl.when(jnp.logical_and(mine, k == core))
-            def _():
-                to_sibling(g, j).wait_recv()
-                part[g, pl.ds(64 * j, 64), :] = (
-                    part[g, pl.ds(64 * j, 64), :].astype(F32) + sib[p].astype(F32)).astype(BF)
-
-                @pl.when(d > 0)
+        @pl.when(k == core)
+        def _():
+            for i in range(2):
+                j = js[i]
+                swap(g, j, i).wait_recv()
+                part[g, pl.ds(64 * j, 64), feats(k)] = (
+                    part[g, pl.ds(64 * j, 64), feats(k)].astype(F32) + sib7[i].astype(F32)).astype(BF)
+
+                @pl.when(away(g, j))
                 def _():
-                    q = 2 * (d == 2).astype(jnp.int32) + (d == 3).astype(jnp.int32)
-                    dev = {"row": r, "col": ((y + d) % 4) * 2 + k}
-                    remote(rows(g, j), fin.at[o, q], y_s.at[0], fin_r.at[o, q], dev).start()
+                    half_to_owner(g, j, i).start()
 
     def early(g, js, core):
         for j in js:
@@ -222,29 +238,40 @@
 
             @pl.when(jnp.logical_and(mine, d == 0))
             def _():
-                t = part[g, pl.ds(64 * j, 64), :].astype(F32)
-                for q in range(3 if (g, j) in DIRECT else 2):
-                    remote(fin.at[o, q], fin.at[o, q], y_s.at[0], fin_r.at[o, q], up).wait_recv()
-                    t = t + fin[o, q].astype(F32)
-                gin_o[pl.ds(pl.multiple_of(o * 64, 64), 64), :] = t.astype(BF)
+                out = pl.ds(pl.multiple_of(o * 64, 64), 64)
+                if (g, j) in DIRECT:
+                    theirs = fin.at[o, 3, :, feats(1 - k)]
+                    remote(theirs, theirs, y_s.at[0], fin_r.at[o, 3], up).wait_recv()
+                    for q in range(3):
+                        remote(fin.at[o, q], fin.at[o, q], y_s.at[0], fin_r.at[o, q], up).wait_recv()
+                    for f, t in ((feats(k), part[g, pl.ds(64 * j, 64), feats(k)]),
+                                 (feats(1 - k), fin[o, 3, :, feats(1 - k)])):
+                        t = t.astype(F32)
+                        for q in range(3):
+                            t = t + fin[o, q, :, f].astype(F32)
+                        gin_o[out, f] = t.astype(BF)
+                else:
+                    t = part[g, pl.ds(64 * j, 64), :].astype(F32)
+                    for q in range(2):
+                        remote(fin.at[o, q], fin.at[o, q], y_s.at[0], fin_r.at[o, q], up).wait_recv()
+                        t = t + fin[o, q].astype(F32)
+                    gin_o[out, :] = t.astype(BF)
 
     def sent(ref, sem):
         remote(ref, ref, sem, x_r.at[0], other).wait_send()
 
     def last_partial(g, js):
         lo, n_rows = 64 * js[0], 64 * len(js)
-        for q in (0, 1):
-            f = pl.ds(512 * q, 512)
+
+        def tile(f):
             part[g, pl.ds(lo, n_rows), f] = lax.dot_general(
                 G[pl.ds(g * 256 + lo, n_rows), :], nw_o[f, :], NT,
                 preferred_element_type=F32).astype(BF)
-            for j in js:
-                p, _, _, mine, _ = place(g, j)
-
-                @pl.when(jnp.logical_not(mine))
-                def _():
-                    remote(part.at[g, pl.ds(64 * j, 64), f], sib.at[p, :, f],
-                           x_s.at[0], x_r.at[p], other).start()
+
+        tile(feats(1 - k))
+        for i in range(2):
+            swap(g, js[i], i).start()
+        tile(feats(k))
 
     def partial(g, lo=0, n_rows=256):
         def tile(n, _):
@@ -311,9 +338,10 @@
     partial(2)
     step1(2)
     recv("PF")
-    send("S", 2)
+    send("S", 2, half=(0,))
+    send("S", -1, half=(0,))
     send("F", 0, half=(1,))
-    send("S", -1)
+    send("S", 2, half=(1,))
     partial(0)
     step1(0)
     step2(2)
@@ -332,74 +360,96 @@
     step3(2)
     step2(1, (0, 1))
     recv("S", 1)
-    send("F", 1)
+    send("F", 1, half=(1,))
+    send("S", -1, half=(1,))
+    send("F", 1, half=(0,))
     partial(3)
     step1(3)
     grad_w((0, 1), 2, 4)
     step2(1, (2, 3))
     step3(0)
     step2(3)
-    recv("S", 2)
-    send("F", 2)
+    grad_w((2, 3), 0, 2)
+    step3(1, (0,))
+    recv("S", 2, half=(0,))
+    send("F", 2, half=(0,))
+    grad_w((2, 3), 2, 4)
+    step3(1, (1,))
+    recv("S", 2, half=(1,))
+    send("F", 2, half=(1,))
     partial(4)
     step1(4)
-    step3(1, (0,))
-    grad_w((2, 3, 4), 0, 1)
-    step3(1, (1,))
-    step2(4)
     step3(3)
-    grad_w((2, 3, 4), 1, 3)
+    step3(1, (2,))
     recv("S", -1, half=(0,))
     send("F", -1, half=(0,))
     send("F", 0, half=(0,))
-    step3(1, (2,))
-    grad_w((2, 3, 4), 3, 4)
+    recv("F", 0, half=(1,))
+    recv("F", 1, half=(1,))
+    partial(5)
+    step1(5)
+    step2(4)
+    grad_w((4, 5), 0, 2)
+    step3(1, (3,))
+    step2(5)
+    grad_w((4, 5), 2, 4)
+    step3(4)
     recv("S", -1, half=(1,))
     send("F", -1, half=(1,))
     recv("F", 1, half=(0,))
-    recv("F", 0, half=(1,))
-    partial(5)
-    step1(5)
-    step3(4)
-    step3(1, (3,))
     recv("F", 2, half=(0,))
-    recv("F", 1, half=(1,))
     partial(6)
     step1(6)
-    step2(5)
     for g in (2, 0):
         step4(g)
+    step3(5)
+    step2(6, core=0)
     recv("F", -1, half=(0,))
     recv("F", 2, half=(1,))
     partial(7, 0, 128)
     step1(7, (0, 1))
-    step2(6)
+    step2(6, core=1)
     recv("F", 0, half=(0,))
     recv("F", -1, half=(1,))
-    step3(5)
     step2(7, (0, 1), 0)
     last_partial(7, (2, 3))
     direct(7, (2, 3), 0)
+    step3(6, core=0)
     locals_[4].wait()
-    grad_w((5, 6, 7), 0, 1)
+    grad_w((6, 7), 0, 1)
     step2(7, (0, 1), 1)
-    step3(6)
-    grad_w((5, 6, 7), 1, 2)
     direct(7, (2, 3), 1)
-    grad_w((5, 6, 7), 2, 3)
-    step3(7, (0, 1))
-    grad_w((5, 6, 7), 3, 4)
+    grad_w((6, 7), 1, 2)
+    step3(7, (0, 1), 0)
+    step3(6, core=1)
+    grad_w((6, 7), 2, 4)
+    step3(7, (0, 1), 1)
     sent(G.at[pl.ds(0, 1920), :], ag_s.at[0])
     sent(A.at[pl.ds(0, 1792), :], at_s.at[0])
-    sent(sib, x_s.at[0])
+    sent(sib7, x7_s.at[0])
+    apart = sum(jnp.logical_not(place(g, j)[3]).astype(jnp.int32) for g, j in DIRECT)
+    for n in range(3):
+        @pl.when(apart == n)
+        def _():
+            sent(sib.at[pl.ds(0, 16 - n)], x_s.at[0])
+
     for g in (1, 3, 4, 5, 6, 7):
         step4(g)
-    sent(sib.at[pl.ds(0, 12)], y_s.at[0])
+    for i, (g, j) in enumerate(DIRECT):
+        @pl.when(away(g, j))
+        def _():
+            half_to_owner(g, j, i).wait_send()
+
+    left = sum(jnp.logical_and(place(g, j)[3], place(g, j)[2] > 0).astype(jnp.int32) for g, j in DIRECT)
+    for n in range(3):
+        @pl.when(left == n)
+        def _():
+            sent(sib.at[pl.ds(0, 12 - n)], y_s.at[0])
 
 
 def store(gin, nw, nm, gin_o, nw_o, nm_o, sem):
     copies = []
-    for src, dst, n in ((nw, nw_o, 8), (nm, nm_o, 8), (gin, gin_o, 1)):
+    for src, dst, n in ((nw, nw_o, 1), (nm, nm_o, 1), (gin, gin_o, 1)):
         step = src.shape[0] // n
         for i in range(n):
             f = pl.ds(i * step, step)
@@ -427,13 +477,14 @@
             pltpu.VMEM((2048, 2048), BF),
             pltpu.VMEM((2048, 1024), BF),
             pltpu.VMEM((1024, 2048), F32),
-            pltpu.VMEM((768, 1024), BF),
+            pltpu.VMEM((512, 1024), BF),
             pltpu.VMEM((8, 256, 1024), BF),
             pltpu.VMEM((16, 64, 1024), BF),
             pltpu.VMEM((8, 64, 512), BF),
-            pltpu.VMEM((4, 3, 64, 1024), BF),
+            pltpu.VMEM((4, 4, 64, 1024), BF),
+            pltpu.VMEM((2, 64, 512), BF), dma((1,)), dma((2,)), dma((2,)),
             dma((1,)), dma((20,)), dma((1,)), dma((11,)),
-            dma((1,)), dma((16,)), dma((1,)), dma((8,)), dma((4, 3)), dma((5,)),
+            dma((1,)), dma((16,)), dma((1,)), dma((8,)), dma((4, 4)), dma((5,)),
         ],
         compiler_params=pltpu.CompilerParams(
             collective_id=0, has_side_effects=True, vmem_limit_bytes=52428800),
@@ -448,7 +499,7 @@
         ),
         in_specs=[vmem] * 3,
         out_specs=(hbm,) * 3,
-        scratch_shapes=[dma((17,))],
+        scratch_shapes=[dma((3,))],
         compiler_params=pltpu.CompilerParams(vmem_limit_bytes=1 << 20),
     )(*[pltpu.with_memory_space_constraint(r, pltpu.VMEM) for r in results])
 

time: 65.9 us -> 64.8 us (0.983)
  Pallas kernels: 64.9 us -> 63.9 us
    pallas_call x1, Pallas kernels: 61.3 us -> 60.4 us  [shards(): pl.pallas_call(kernel, out_shape=(pltpu.VMEM((256, 1024), BF), pltpu.VMEM...]
where the time goes in v5:
time: 64.8 us; the launch traced here: 64.7 us
  Pallas kernels  63.9 us (99%)
  between operations  0.8 us (1%)
    pallas_call x1, Pallas kernels, shards(): pl.pallas_call(kernel, out_shape=(pltpu.VMEM((256, 1024), BF), pltpu.VMEM...  60.4 us
    pallas_call x1, Pallas kernels, shards(): pl.pallas_call(store, out_shape=(jax.ShapeDtypeStruct((256, 1024), BF), j...  3.46 us

profile of v5, /device:TPU:1, one launch (start us, length us, event | category | flops | bytes accessed | tf_op | source)
XLA Modules:
  0.0 64.7 jit_solution(7601258360173406621)
XLA Ops:
  0.6 60.4 %shard_map.67 = (bf16[256,1024]{1,0:T(8,128)(2,1)S(1)}, bf16[1024,2048]{1,0:T(8,128)(2,1)S(1)}, bf16[1024,2048]{1,0:T(8,128)(2,1)S(1)}) custom-call(bf16[256,1024]{1,0:T(8,128)(2,1)} %attn.1, bf16[128,2048]{1,0:T(8,128)(2,1)} %gout.1, bf16[1024,2048]{1,0:T(8,128)(2,1)} %w_in.1, bf16[1024,2048]{1,0:T(8,128)(2,1)} %m_in.1), custom_call_target="tpu_custom_call" | custom-call | flops 17179869184 | bytes 17825792 | tf_op jit(solution)/shard_map/pallas_call | solution.py:467
  61.0 3.5 %shard_map.68 = (bf16[256,1024]{1,0:T(8,128)(2,1)}, bf16[1024,2048]{1,0:T(8,128)(2,1)}, bf16[1024,2048]{1,0:T(8,128)(2,1)}) custom-call(bf16[256,1024]{1,0:T(8,128)(2,1)S(1)} %get-tuple-element.6.gin, bf16[1024,2048]{1,0:T(8,128)(2,1)S(1)} %get-tuple-element.7.nw, bf16[1024,2048]{1,0:T(8,128)(2,1)S(1)} %get-tuple-element.8.nm), custom_call_target="tpu_custom_call" | custom-call | tf_op jit(solution)/shard_map/pallas_call | solution.py:493

commit v6 on v5

--- a/solution.py
+++ b/solution.py
@@ -97,6 +97,12 @@
                 landed = slot((h, 2, 0) if kind == "PF" else (h, *rest, 2))
             sem = ag_r.at[waits.index((kind, h, *rest))]
             remote(landed, landed, ag_s.at[0], sem, other).wait_recv()
+
+    def relay(core):
+        @pl.when(k == core)
+        def _():
+            recv("S", -1, half=(1,))
+            send("F", -1, half=(1,))
 
     def block(dy, dk=0, lo=0, n=256):
         col = ((y + dy + 4) % 4) * 2 + (k + dk) % 2
@@ -392,10 +398,10 @@
     grad_w((4, 5), 0, 2)
     step3(1, (3,))
     step2(5)
+    relay(1)
     grad_w((4, 5), 2, 4)
     step3(4)
-    recv("S", -1, half=(1,))
-    send("F", -1, half=(1,))
+    relay(0)
     recv("F", 1, half=(0,))
     recv("F", 2, half=(0,))
     partial(6)
@@ -416,14 +422,15 @@
     direct(7, (2, 3), 0)
     step3(6, core=0)
     locals_[4].wait()
+    step2(7, (0, 1), 1)
     grad_w((6, 7), 0, 1)
-    step2(7, (0, 1), 1)
     direct(7, (2, 3), 1)
     grad_w((6, 7), 1, 2)
     step3(7, (0, 1), 0)
     step3(6, core=1)
-    grad_w((6, 7), 2, 4)
+    grad_w((6, 7), 2, 3)
     step3(7, (0, 1), 1)
+    grad_w((6, 7), 3, 4)
     sent(G.at[pl.ds(0, 1920), :], ag_s.at[0])
     sent(A.at[pl.ds(0, 1792), :], at_s.at[0])
     sent(sib7, x7_s.at[0])

time: 64.8 us -> 64.9 us (level)
  no operation moved by 1% of the time
where the time goes in v6:
time: 64.9 us; the launch traced here: 64.8 us
  Pallas kernels  64 us (99%)
  between operations  0.8 us (1%)
    pallas_call x1, Pallas kernels, shards(): pl.pallas_call(kernel, out_shape=(pltpu.VMEM((256, 1024), BF), pltpu.VMEM...  60.6 us
    pallas_call x1, Pallas kernels, shards(): pl.pallas_call(store, out_shape=(jax.ShapeDtypeStruct((256, 1024), BF), j...  3.46 us

profile of v6, /device:TPU:1, one launch (start us, length us, event | category | flops | bytes accessed | tf_op | source)
XLA Modules:
  0.0 64.8 jit_solution(16502818317710306179)
XLA Ops:
  0.6 60.6 %shard_map.67 = (bf16[256,1024]{1,0:T(8,128)(2,1)S(1)}, bf16[1024,2048]{1,0:T(8,128)(2,1)S(1)}, bf16[1024,2048]{1,0:T(8,128)(2,1)S(1)}) custom-call(bf16[256,1024]{1,0:T(8,128)(2,1)} %attn.1, bf16[128,2048]{1,0:T(8,128)(2,1)} %gout.1, bf16[1024,2048]{1,0:T(8,128)(2,1)} %w_in.1, bf16[1024,2048]{1,0:T(8,128)(2,1)} %m_in.1), custom_call_target="tpu_custom_call" | custom-call | flops 17179869184 | bytes 17825792 | tf_op jit(solution)/shard_map/pallas_call | solution.py:474
  61.2 3.5 %shard_map.68 = (bf16[256,1024]{1,0:T(8,128)(2,1)}, bf16[1024,2048]{1,0:T(8,128)(2,1)}, bf16[1024,2048]{1,0:T(8,128)(2,1)}) custom-call(bf16[256,1024]{1,0:T(8,128)(2,1)S(1)} %get-tuple-element.6.gin, bf16[1024,2048]{1,0:T(8,128)(2,1)S(1)} %get-tuple-element.7.nw, bf16[1024,2048]{1,0:T(8,128)(2,1)S(1)} %get-tuple-element.8.nm), custom_call_target="tpu_custom_call" | custom-call | tf_op jit(solution)/shard_map/pallas_call | solution.py:500
